TPU v7x, 32 devices: a whole 2x2x4 slice. The times are simulated.
32 devices in a mesh: dp: 8 (over y, x, core), mp: 4 (over z).
Axes of the slice: x: 2, y: 2, z: 4, core: 2. Of those that a mesh axis runs over, the one named last changes fastest.
Arguments:
- states: bfloat16 [512, 64, 256], P('dp', 'mp'), may hold values from -6 to 6
- key_embed: bfloat16 [512, 128], P('dp'), may hold values from -6 to 6
- partner: int32 [512], replicated, may hold values from 0 to 511, as said below
- mix_numer: int32 [512], P('dp'), may hold values from 1 to 15
- lengths: int32 [512], replicated, may hold values from 8 to 64
- w_qkv: bfloat16 [3, 256, 256], P(None, None, 'mp'), may hold values from -0.375 to 0.375
- w_out: bfloat16 [256, 256], P('mp'), may hold values from -0.375 to 0.375
- w_up: bfloat16 [256, 1024], P(None, 'mp'), may hold values from -0.375 to 0.375
- w_down: bfloat16 [1024, 256], P('mp'), may hold values from -0.1875 to 0.1875
- w_proj: bfloat16 [256, 128], replicated, may hold values from -0.375 to 0.375
Outputs:
- session_loss: float32 [512], P('dp')
- grad_states: float32 [512, 64, 256], P('dp', 'mp')
Inputs may be any that keep to these rules, and one draw needn't show every extreme that they name: partner is a permutation of the 512 sessions; a session and its partner lie in different aligned blocks of 64 sessions, and at most 10 sessions of one block have their partners in one same other block.
All inputs are finite; a program needn't handle non-finite values.
Results may differ from a plain program's by a relative error of at most 0.0091.
Values may be sent and summed in bfloat16 or wider, within the bound.
A program may use at most 64 MiB of HBM per device.

v0:
```python
import jax
import jax.numpy as jnp
from jax import lax
from jax.sharding import PartitionSpec as P

HD = 64
SOFTMAX_TEMP = 0.1
LN_EPS = 1e-05
NORM_EPS = 1e-06
TOP_PRECISION = lax.Precision.HIGHEST


def swap_rows(buffer):
    return lax.all_to_all(buffer, "dp", split_axis=0, concat_axis=0, tiled=True)


def local(states, key_embed, partner, mix_numer, lengths, w_qkv, w_out, w_up, w_down, w_proj):
    sessions_dev, ev_part, width = states.shape
    n_data = lax.axis_size("dp")
    capacity = (sessions_dev + n_data - 2) // (n_data - 1)
    device_index = lax.axis_index("dp")
    model_index = lax.axis_index("mp")
    all_keys = lax.all_gather(key_embed, "dp", axis=0, tiled=True)
    session_count = partner.shape[0]
    local_ids = jnp.arange(sessions_dev, dtype=jnp.int32)
    own_ids = device_index * sessions_dev + local_ids
    own_partner = lax.dynamic_slice_in_dim(partner, device_index * sessions_dev, sessions_dev)
    mixup_weight = mix_numer.astype(jnp.float32) / 16.0
    source = own_partner // sessions_dev
    earlier = local_ids[None, :] < local_ids[:, None]
    in_slot = jnp.sum(((source[:, None] == source[None, :]) & earlier).astype(jnp.int32), axis=1)
    wanted = partner[None, :] == own_ids[:, None]
    seeker = jnp.sum(
        jnp.where(wanted, jnp.arange(session_count, dtype=jnp.int32)[None, :], 0), axis=1
    )
    target = seeker // sessions_dev
    seeker_rows = partner.reshape(n_data, sessions_dev)[target]
    out_slot = jnp.sum(
        (
            (seeker_rows // sessions_dev == device_index)
            & (local_ids[None, :] < (seeker % sessions_dev)[:, None])
        ).astype(jnp.int32),
        axis=1,
    )
    row_len = ev_part * width
    outgoing = (
        jnp.zeros((n_data, capacity, row_len), jnp.bfloat16)
        .at[target, out_slot]
        .set(states.reshape(sessions_dev, row_len))
    )
    incoming = swap_rows(outgoing)
    partner_states = incoming[source, in_slot].reshape(sessions_dev, ev_part, width)
    mix_rows = mixup_weight[:, None, None]
    mixed_part = (
        mix_rows * states.astype(jnp.float32)
        + (1.0 - mix_rows) * partner_states.astype(jnp.float32)
    ).astype(jnp.bfloat16)
    own_lengths = lax.dynamic_slice_in_dim(lengths, device_index * sessions_dev, sessions_dev)
    len_mix = jnp.maximum(own_lengths, lengths[own_partner])
    qkv_full, out_full, up_full, down_full = (w_qkv, w_out, w_up, w_down)
    mixed = lax.all_gather(mixed_part, "mp", axis=1, tiled=True)
    layer_sessions = mixed.shape[0]
    events = mixed.shape[1]
    rows = layer_sessions * events
    positions = jnp.arange(events, dtype=jnp.int32)
    token_mask = (positions[None, :] < len_mix[:, None]).astype(jnp.float32)
    pool_weights = token_mask / len_mix[:, None].astype(jnp.float32)
    inputs_f = mixed.astype(jnp.float32).reshape(rows, width)
    row_mean = jnp.mean(inputs_f, axis=1, keepdims=True)
    centered = inputs_f - row_mean
    inv_std = lax.rsqrt(jnp.mean(centered * centered, axis=1, keepdims=True) + LN_EPS)
    unit_rows = centered * inv_std
    normed = unit_rows.astype(jnp.bfloat16)
    projected = jnp.einsum(
        "rd,jdf->jrf", normed, qkv_full, preferred_element_type=jnp.float32
    ).astype(jnp.bfloat16)
    inner_part = qkv_full.shape[2]
    heads_part = inner_part // HD
    query_h = projected[0].reshape(layer_sessions, events, heads_part, HD)
    key_h = projected[1].reshape(layer_sessions, events, heads_part, HD)
    value_h = projected[2].reshape(layer_sessions, events, heads_part, HD)
    score_scale = HD ** (-0.5)
    scores = (
        jnp.einsum("sthc,srhc->shtr", query_h, key_h, preferred_element_type=jnp.float32)
        * score_scale
    )
    exp_scores = jnp.exp(scores) * token_mask[:, None, None, :]
    probs = exp_scores / jnp.sum(exp_scores, axis=3, keepdims=True)
    probs_b = probs.astype(jnp.bfloat16)
    context = (
        jnp.einsum("shtr,srhc->sthc", probs_b, value_h, preferred_element_type=jnp.float32)
        .astype(jnp.bfloat16)
        .reshape(rows, inner_part)
    )
    pre_act = jnp.dot(normed, up_full, preferred_element_type=jnp.float32)
    hidden = jax.nn.gelu(pre_act).astype(jnp.bfloat16)
    branch = jnp.dot(context, out_full, preferred_element_type=jnp.float32) + jnp.dot(
        hidden, down_full, preferred_element_type=jnp.float32
    )
    pooled_branch = jnp.einsum(
        "st,std->sd",
        pool_weights,
        branch.reshape(layer_sessions, events, width),
        precision=TOP_PRECISION,
    )
    pooled_input = jnp.einsum(
        "st,std->sd",
        pool_weights,
        inputs_f.reshape(layer_sessions, events, width),
        precision=TOP_PRECISION,
    )
    pooled = lax.psum(pooled_branch, "mp") + pooled_input
    proj_f = w_proj.astype(jnp.float32)
    embed = jnp.dot(pooled, proj_f, precision=TOP_PRECISION)
    inv_norm = lax.rsqrt(jnp.sum(embed * embed, axis=1, keepdims=True) + NORM_EPS)
    unit_query_rows = embed * inv_norm
    keys_f = all_keys.astype(jnp.float32)
    unit_key_rows = keys_f * lax.rsqrt(jnp.sum(keys_f * keys_f, axis=1, keepdims=True) + NORM_EPS)
    pair_logits = (
        jnp.einsum("an,qn->aq", unit_query_rows, unit_key_rows, precision=TOP_PRECISION)
        / SOFTMAX_TEMP
    )
    exp_logits = jnp.exp(pair_logits)
    sum_exp = jnp.sum(exp_logits, axis=1)
    own_logit = jnp.take_along_axis(pair_logits, own_ids[:, None], axis=1)[:, 0]
    partner_logit = jnp.take_along_axis(pair_logits, own_partner[:, None], axis=1)[:, 0]
    session_loss = (
        jnp.log(sum_exp) - mixup_weight * own_logit - (1.0 - mixup_weight) * partner_logit
    )
    normalized_exponent = exp_logits / sum_exp[:, None]
    unit_gradient = (
        jnp.dot(normalized_exponent, unit_key_rows, precision=TOP_PRECISION)
        - mixup_weight[:, None] * unit_key_rows[own_ids]
        - (1.0 - mixup_weight)[:, None] * unit_key_rows[own_partner]
    ) / SOFTMAX_TEMP
    grad_embed = (
        unit_gradient
        - unit_query_rows * jnp.sum(unit_query_rows * unit_gradient, axis=1, keepdims=True)
    ) * inv_norm
    grad_pooled = jnp.einsum("se,de->sd", grad_embed, proj_f, precision=TOP_PRECISION)
    grad_full = grad_pooled[:, None, :] * pool_weights[:, :, None]
    grad_b = grad_full.reshape(rows, width).astype(jnp.bfloat16)
    d_hidden = jnp.einsum("rd,fd->rf", grad_b, down_full, preferred_element_type=jnp.float32)
    d_pre = jax.vjp(jax.nn.gelu, pre_act)[1](d_hidden)[0].astype(jnp.bfloat16)
    d_context = (
        jnp.einsum("rd,fd->rf", grad_b, out_full, preferred_element_type=jnp.float32)
        .astype(jnp.bfloat16)
        .reshape(layer_sessions, events, heads_part, HD)
    )
    d_value = jnp.einsum(
        "shtr,sthc->srhc", probs_b, d_context, preferred_element_type=jnp.float32
    ).astype(jnp.bfloat16)
    d_prob = jnp.einsum("sthc,srhc->shtr", d_context, value_h, preferred_element_type=jnp.float32)
    d_score = (
        probs * (d_prob - jnp.sum(probs * d_prob, axis=3, keepdims=True)) * score_scale
    ).astype(jnp.bfloat16)
    d_query = jnp.einsum(
        "shtr,srhc->sthc", d_score, key_h, preferred_element_type=jnp.float32
    ).astype(jnp.bfloat16)
    d_key = jnp.einsum(
        "shtr,sthc->srhc", d_score, query_h, preferred_element_type=jnp.float32
    ).astype(jnp.bfloat16)
    d_proj = jnp.stack([d_query, d_key, d_value]).reshape(3, rows, inner_part)
    d_normed = jnp.einsum(
        "jrf,jdf->rd", d_proj, qkv_full, preferred_element_type=jnp.float32
    ) + jnp.einsum("rf,df->rd", d_pre, up_full, preferred_element_type=jnp.float32)
    d_normed = d_normed.reshape(layer_sessions, events, width)
    unit_all = unit_rows.reshape(layer_sessions, events, width)
    inv_all = inv_std.reshape(layer_sessions, events, 1)
    event_start = model_index * ev_part
    unit_part = lax.dynamic_slice_in_dim(unit_all, event_start, ev_part, 1)
    inv_part = lax.dynamic_slice_in_dim(inv_all, event_start, ev_part, 1)
    d_full = lax.psum(d_normed, "mp")
    d_local = lax.dynamic_slice_in_dim(d_full, event_start, ev_part, 1)
    center = jnp.mean(d_local, axis=2, keepdims=True)
    along = jnp.mean(d_local * unit_part, axis=2, keepdims=True)
    d_mixed = (
        lax.dynamic_slice_in_dim(grad_full, event_start, ev_part, 1)
        + (d_local - center - unit_part * along) * inv_part
    )
    d_mixed_rows = d_mixed.reshape(sessions_dev, row_len)
    back_rows = ((1.0 - mixup_weight)[:, None] * d_mixed_rows).astype(jnp.bfloat16)
    returning = (
        jnp.zeros((n_data, capacity, row_len), jnp.bfloat16).at[source, in_slot].set(back_rows)
    )
    arrived = swap_rows(returning)
    grad_states = mixup_weight[:, None] * d_mixed_rows + arrived[target, out_slot].astype(
        jnp.float32
    )
    return (session_loss, grad_states.reshape(sessions_dev, ev_part, width))


def solution(mesh):
    placed = (
        P("dp", "mp", None),
        P("dp", None),
        P(),
        P("dp"),
        P(),
        P(None, None, "mp"),
        P("mp", None),
        P(None, "mp"),
        P("mp", None),
        P(),
    )
    return jax.shard_map(
        local, mesh=mesh, in_specs=placed, out_specs=(P("dp"), P("dp", "mp", None)), check_vma=False
    )
```

profile of v0, /device:TPU:0, one launch (start us, length us, event | category | flops | bytes accessed | tf_op | source)
XLA Modules:
  0.0 415.0 jit_solution(1312834488764694528)
XLA Ops:
  8.9 1.3 fusion.104
  11.0 1.2 copy.88
  12.3 9.7 %scatter_fusion = bf16[8,10,4096]{2,0,1:T(8,128)(2,1)S(1)} fusion(bf16[8,10,4096]{2,0,1:T(8,128)(2,1)S(1)} %broadcast.348.clone, s32[64]{0:T(128)S(1)} %get-tuple-element.15, bf16[64,4096]{1,0:T(8,128)(2,1)S(1)} %bitcast.216), kind=kCustom, calls=%fused_computation.8 | custom fusion | bytes 1573376 | tf_op jit(solution)/shard_map/scatter | solution.py:49
  22.0 1.4 copy.60
  23.4 5.2 %all-to-all-start = ((bf16[8,10,4096]{2,1,0:T(8,128)(2,1)}), bf16[8,10,4096]{2,1,0:T(8,128)(2,1)S(1)}, u32[]{:S(2)}, u32[]{:S(2)}) async-start(bf16[8,10,4096]{2,1,0:T(8,128)(2,1)} %copy.60), calls=%async_computation | async-start | bytes 2097152 | tf_op jit(solution)/shard_map/all_to_all | solution.py:14
  28.8 15.1 %all-to-all-done = bf16[8,10,4096]{2,1,0:T(8,128)(2,1)S(1)} async-done(((bf16[8,10,4096]{2,1,0:T(8,128)(2,1)}), bf16[8,10,4096]{2,1,0:T(8,128)(2,1)S(1)}, u32[]{:S(2)}, u32[]{:S(2)}) %all-to-all-start) | async-done | bytes 655392 | tf_op jit(solution)/shard_map/all_to_all | solution.py:14
  44.3 2.2 gather_fusion.2
  49.5 8.2 %all_gather.7 = bf16[512,128]{1,0:T(8,128)(2,1)S(1)} all-gather(bf16[64,128]{1,0:T(8,128)(2,1)S(1)} %copy-done.17), channel_id=1, replica_groups=mesh['dp'=8,'mp'=4] {'dp'}, dimensions={0}, use_global_device_ids=true | all-gather | bytes 147456 | tf_op jit(solution)/shard_map/all_gather | solution.py:23
  59.2 1.2 gather_fusion.3
  61.1 31.9 %all-gather.2.cloned.1.call-done = bf16[64,64,256]{2,1,0:T(8,128)(2,1)} async-done(((bf16[64,16,256]{2,1,0:T(8,128)(2,1)}), bf16[64,64,256]{2,1,0:T(8,128)(2,1)}) %all-gather.2.cloned.1.call-update) | async-done | bytes 2097168 | tf_op jit(solution)/shard_map/all_gather | solution.py:61
  93.0 2.4 convert_reduce_fusion
  95.4 3.1 broadcast_subtract_fusion
  98.6 2.5 fusion.10
  103.1 2.1 reshape.404
  105.1 2.1 reshape.403
  107.3 1.5 copy.87
  108.9 3.7 fusion.132
  112.6 5.0 %fusion.26 = (f32[64,64]{1,0:T(8,128)S(1)}, f32[64,64,64]{1,2,0:T(8,128)S(1)}) fusion(f32[64,64]{1,0:T(8,128)S(1)} %copy-done.15, bf16[64,64,64]{1,0,2:T(8,128)(2,1)S(1)} %copy-done.9, bf16[64,64,64]{1,0,2:T(8,128)(2,1)S(1)} %copy-done.7), kind=kOutput, calls=%fused_computation.48 | convolution fusion | flops 34336768 | bytes 2129920 | tf_op jit(solution)/shard_map/sthc,srhc->shtr/dot_general | solution.py:84
  117.7 1.3 fusion.44
  121.3 1.4 copy-done.4
  122.7 1.9 convolution_add_fusion.1
  124.7 2.1 fusion.133
  127.7 1.6 fusion.134
  129.2 31.5 %all-reduce.3.cloned.1.call-done = f32[64,256]{1,0:T(8,128)} async-done(((f32[64,256]{1,0:T(8,128)}), f32[64,256]{1,0:T(8,128)}) %all-reduce.3.cloned.1.call-update) | async-done | bytes 65552 | tf_op jit(solution)/shard_map/psum | solution.py:112
  162.5 1.3 multiply_reduce_fusion.3
  164.9 1.4 fusion.8
  166.3 1.6 convolution_convert_fusion
  167.9 2.8 reshape.407
  170.7 3.8 fusion.58
  174.5 3.4 fusion.45
  177.8 6.9 %fusion.49 = bf16[64,64,1,64]{1,3,0,2:T(8,128)(2,1)} fusion(f32[64,64,64]{1,2,0:T(8,128)} %fusion.58, bf16[64,64,64]{1,0,2:T(8,128)(2,1)} %reshape.404, f32[64,64,64]{1,2,0:T(8,128)} %copy-done.27, f32[64,64]{1,0:T(8,128)} %copy-done.29, f32[64,64]{1,0:T(8,128)} %fusion.80), kind=kOutput, calls=%fused_computation.64 | convolution fusion | flops 36704320 | bytes 3178496 | tf_op jit(solution)/shard_map/shtr,srhc->sthc/dot_general | solution.py:157
  184.7 7.8 %fusion.46 = bf16[64,64,1,64]{1,3,0,2:T(8,128)(2,1)} fusion(f32[64,64,64]{1,2,0:T(8,128)} %fusion.58, bf16[64,64,64]{1,0,2:T(8,128)(2,1)S(1)} %copy-done.8, f32[64,64,64]{1,2,0:T(8,128)} %copy-done.27, f32[64,64]{1,0:T(8,128)} %copy-done.29, f32[64,64]{1,0:T(8,128)} %fusion.80), kind=kOutput, calls=%fused_computation.63 | convolution fusion | flops 36704320 | bytes 3178496 | tf_op jit(solution)/shard_map/shtr,sthc->srhc/dot_general | solution.py:160
  192.5 1.9 copy.77
  194.4 1.6 stack.14
  196.1 1.9 copy.74
  198.0 1.6 stack.13
  199.6 1.9 copy.71
  201.5 1.6 stack.12
  203.1 4.1 convolution_bitcast_fusion
  207.3 7.0 %convolution_add_fusion = f32[4096,256]{1,0:T(8,128)} fusion(f32[4096,256]{1,0:T(8,128)} %convolution_bitcast_fusion, bf16[256,256]{1,0:T(8,128)(2,1)S(1)} %copy-done.11, f32[4096,256]{1,0:T(8,128)} %fusion.132, bf16[4096,256]{1,0:T(8,128)(2,1)S(1)} %fusion.8, bf16[256,256]{1,0:T(8,128)(2,1)S(1)} %copy-done), kind=kOutput, calls=%fused_computation.13 | convolution fusion | flops 1095761920 | bytes 14942208 | tf_op jit(solution)/shard_map/rf,df->rd/dot_general | solution.py:166
  214.4 154.6 %all-reduce.5.cloned.1.call-done = f32[64,64,256]{2,1,0:T(8,128)} async-done(((f32[64,64,256]{2,1,0:T(8,128)}), f32[64,64,256]{2,1,0:T(8,128)}) %all-reduce.5.cloned.1.call-update) | async-done | bytes 4194320 | tf_op jit(solution)/shard_map/psum | solution.py:173
  369.1 2.1 dynamic-slice_reduce_fusion
  371.2 2.0 multiply_add_fusion
  374.0 9.7 %scatter_fusion.1 = bf16[8,10,4096]{2,0,1:T(8,128)(2,1)S(1)} fusion(bf16[8,10,4096]{2,0,1:T(8,128)(2,1)S(1)} %broadcast.348, s32[64]{0:T(128)S(1)} %get-tuple-element.16, bf16[64,4096]{1,0:T(8,128)(2,1)S(1)} %multiply_convert_fusion.3), kind=kCustom, calls=%fused_computation.9 | custom fusion | bytes 1573376 | tf_op jit(solution)/shard_map/scatter | solution.py:184
  383.7 1.4 copy.78
  385.1 3.9 all-to-all-start.1
  391.4 13.0 %all-to-all-done.1 = bf16[8,10,4096]{2,1,0:T(8,128)(2,1)S(1)} async-done(((bf16[8,10,4096]{2,1,0:T(8,128)(2,1)}), bf16[8,10,4096]{2,1,0:T(8,128)(2,1)S(1)}, u32[]{:S(2)}, u32[]{:S(2)}) %all-to-all-start.1) | async-done | bytes 655392 | tf_op jit(solution)/shard_map/all_to_all | solution.py:14
  404.7 2.2 gather_fusion.5
  (127 shorter events, 21.3 us)
Async XLA Ops:
  7.2 114.1 %copy-start = (bf16[256,256]{1,0:T(8,128)(2,1)S(1)}, bf16[256,256]{1,0:T(8,128)(2,1)}, u32[]{:S(2)}) copy-start(bf16[256,256]{1,0:T(8,128)(2,1)} %param.20) | copy-start | bytes 393220
  22.0 6.8 %copy-start.25 = (s32[64]{0:T(128)S(1)}, s32[64]{0:T(128)}, u32[]{:S(2)}) copy-start(s32[64]{0:T(128)} %param.15) | copy-start | bytes 772
  23.4 20.6 %all-to-all-start = ((bf16[8,10,4096]{2,1,0:T(8,128)(2,1)}), bf16[8,10,4096]{2,1,0:T(8,128)(2,1)S(1)}, u32[]{:S(2)}, u32[]{:S(2)}) async-start(bf16[8,10,4096]{2,1,0:T(8,128)(2,1)} %copy.60), calls=%async_computation | async-start | bytes 2097152 | tf_op jit(solution)/shard_map/all_to_all | solution.py:14
  28.6 64.4 %all-gather.2.cloned.1.call-start = ((), (), s32[]{:S(2)}) async-start(), calls=%async_computation.2 | async-start | bytes 2621440 | tf_op jit(solution)/shard_map/all_gather | solution.py:61
  28.8 17.9 %copy-start.21 = (f32[64]{0:T(128)}, f32[64]{0:T(128)S(1)}, u32[]{:S(2)}) copy-start(f32[64]{0:T(128)S(1)} %get-tuple-element.21) | copy-start | bytes 772
  28.8 17.9 %copy-start.23 = (f32[64]{0:T(128)}, f32[64]{0:T(128)S(1)}, u32[]{:S(2)}) copy-start(f32[64]{0:T(128)S(1)} %get-tuple-element.20) | copy-start | bytes 772
  44.3 2.4 copy-start.6
  46.5 1.3 copy-start.1
  46.5 3.0 copy-start.17
  47.8 112.9 %all-reduce.3.cloned.1.call-start = ((), (), s32[]{:S(2)}) async-start(), calls=%async_computation.3 | async-start | bytes 131072 | tf_op jit(solution)/shard_map/psum | solution.py:112
  93.0 2.4 copy-start.2
  98.6 2.5 copy-start.14
  108.8 3.8 copy-start.7
  108.8 3.8 copy-start.9
  108.8 3.8 copy-start.15
  117.6 1.4 copy-start.27
  117.7 1.4 copy-start.29
  119.0 1.5 copy-start.12
  120.5 2.2 copy-start.4
  124.7 3.0 copy-start.3
  127.4 33.3 %copy-start.10 = (bf16[256,128]{1,0:T(8,128)(2,1)S(1)}, bf16[256,128]{1,0:T(8,128)(2,1)}, u32[]{:S(2)}) copy-start(bf16[256,128]{1,0:T(8,128)(2,1)} %param.21) | copy-start | bytes 196612
  127.4 241.6 %all-reduce.5.cloned.1.call-start = ((), (), s32[]{:S(2)}) async-start(), calls=%async_computation.4 | async-start | bytes 8388608 | tf_op jit(solution)/shard_map/psum | solution.py:173
  160.7 5.6 %copy-start.13 = (bf16[64,256]{1,0:T(8,128)(2,1)S(1)}, bf16[64,256]{1,0:T(8,128)(2,1)}, u32[]{:S(2)}) copy-start(bf16[64,256]{1,0:T(8,128)(2,1)} %param.18) | copy-start | bytes 98308
  162.5 1.3 copy-start.18
  170.7 3.8 copy-start.5
  170.7 3.8 copy-start.16
  170.7 3.8 copy-start.28
  170.7 3.8 copy-start.30
  177.8 6.9 %copy-start.8 = (bf16[64,64,64]{1,0,2:T(8,128)(2,1)S(1)}, bf16[64,64,64]{1,0,2:T(8,128)(2,1)}, u32[]{:S(2)}) copy-start(bf16[64,64,64]{1,0,2:T(8,128)(2,1)} %reshape.403) | copy-start | bytes 1572868
  203.1 4.1 copy-start.11
  371.2 2.6 copy-start.22
  383.7 5.4 %copy-start.20 = (s32[64,1,1]{0,2,1:T(1,128)S(1)}, s32[64,1,1]{0,2,1:T(1,128)}, u32[]{:S(2)}) copy-start(s32[64,1,1]{0,2,1:T(1,128)} %get-tuple-element.5) | copy-start | bytes 772
  383.7 7.2 %copy-start.19 = (f32[64]{0:T(128)S(1)}, f32[64]{0:T(128)}, u32[]{:S(2)}) copy-start(f32[64]{0:T(128)} %copy-done.18) | copy-start | bytes 772
  383.7 7.2 %copy-start.26 = (s32[64]{0:T(128)S(1)}, s32[64]{0:T(128)}, u32[]{:S(2)}) copy-start(s32[64]{0:T(128)} %param.15) | copy-start | bytes 772
  385.1 19.3 %all-to-all-start.1 = ((bf16[8,10,4096]{2,1,0:T(8,128)(2,1)}), bf16[8,10,4096]{2,1,0:T(8,128)(2,1)S(1)}, u32[]{:S(2)}, u32[]{:S(2)}) async-start(bf16[8,10,4096]{2,1,0:T(8,128)(2,1)} %copy.78), calls=%async_computation.1 | async-start | bytes 2097152 | tf_op jit(solution)/shard_map/all_to_all | solution.py:14
  404.7 2.4 copy-start.24
Sparse Core Ops, SparseCore 0:
  47.9 45.0 all-gather.1
  127.6 33.0 all-reduce.2
  214.4 154.6 all-reduce.4
where the time goes:
time: 422 us; the launch traced here: 415 us
  waiting for transfers between devices  246 us (58%)
  local copies, waits for them, and re-layouts  60.4 us (14%)
  matrix products  55.9 us (13%)
  other arithmetic  20.1 us (5%)
  between operations  14.7 us (3%)
  starting transfers between devices  9.43 us (2%)
  blocking collectives  8.24 us (2%)
    psum x1, waiting for transfers between devices, local(): d_full = lax.psum(d_normed, 'mp')  155 us
    all_gather x1, waiting for transfers between devices, local(): mixed = lax.all_gather(mixed_part, 'mp', axis=1, tiled=True)  31.9 us
    psum x1, waiting for transfers between devices, local(): pooled = lax.psum(pooled_branch, 'mp') + pooled_input  31.5 us
    all_to_all x2, waiting for transfers between devices, swap_rows(): return lax.all_to_all(buffer, 'dp', split_axis=0, concat_axis=0, tiled=True)  28.1 us
    scatter x2, local copies, waits for them, and re-layouts, local(): outgoing = jnp.zeros((n_data, capacity, row_len), jnp.bfloat16).at[target...  11.1 us
    scatter x2, local copies, waits for them, and re-layouts, local(): jnp.zeros((n_data, capacity, row_len), jnp.bfloat16).at[source, in_slot]  11.1 us
    all_to_all x2, starting transfers between devices, swap_rows(): return lax.all_to_all(buffer, 'dp', split_axis=0, concat_axis=0, tiled=True)  9.13 us
    another operation x6, local copies, waits for them, and re-layouts  8.6 us
  transfers between devices with their start and end apart: 5, of which 5 were waited for; matrix products, arithmetic and copies ran while one was open for 2% of the time, Pallas kernels for 0%

commit v1 on v0

--- a/solution.py
+++ b/solution.py
@@ -109,7 +109,7 @@
         inputs_f.reshape(layer_sessions, events, width),
         precision=TOP_PRECISION,
     )
-    pooled = lax.psum(pooled_branch, "mp") + pooled_input
+    pooled = jnp.sum(lax.all_gather(pooled_branch, "mp"), axis=0) + pooled_input
     proj_f = w_proj.astype(jnp.float32)
     embed = jnp.dot(pooled, proj_f, precision=TOP_PRECISION)
     inv_norm = lax.rsqrt(jnp.sum(embed * embed, axis=1, keepdims=True) + NORM_EPS)

time: 422 us -> 402 us (0.953)
  waiting for transfers between devices: 246 us -> 214 us
  blocking collectives: 8.24 us -> 23.2 us
    psum x1 -> x0, waiting for transfers between devices: 31.5 us -> none  [local(): pooled = lax.psum(pooled_branch, 'mp') + pooled_input]
    all_gather x0 -> x1, blocking collectives: none -> 14.9 us  [local(): pooled = jnp.sum(lax.all_gather(pooled_branch, 'mp'), axis=0) + pooled_input]
  transfers between devices with their start and end apart: 5 -> 4, of which waited for: 5 -> 4; matrix products, arithmetic and copies ran while one was open for 2% -> 2% of each run, Pallas kernels for 0% -> 0%
where the time goes in v1:
time: 402 us; the launch traced here: 395 us
  waiting for transfers between devices  214 us (53%)
  local copies, waits for them, and re-layouts  59.9 us (15%)
  matrix products  53.3 us (13%)
  blocking collectives  23.2 us (6%)
  other arithmetic  21 us (5%)
  between operations  15.1 us (4%)
  starting transfers between devices  9.21 us (2%)
    psum x1, waiting for transfers between devices, local(): d_full = lax.psum(d_normed, 'mp')  154 us
    all_gather x1, waiting for transfers between devices, local(): mixed = lax.all_gather(mixed_part, 'mp', axis=1, tiled=True)  31.9 us
    all_to_all x2, waiting for transfers between devices, swap_rows(): return lax.all_to_all(buffer, 'dp', split_axis=0, concat_axis=0, tiled=True)  28.1 us
    all_gather x1, blocking collectives, local(): pooled = jnp.sum(lax.all_gather(pooled_branch, 'mp'), axis=0) + pooled_input  14.9 us
    scatter x2, local copies, waits for them, and re-layouts, local(): outgoing = jnp.zeros((n_data, capacity, row_len), jnp.bfloat16).at[target...  11.1 us
    scatter x2, local copies, waits for them, and re-layouts, local(): jnp.zeros((n_data, capacity, row_len), jnp.bfloat16).at[source, in_slot]  11.1 us
    all_to_all x2, starting transfers between devices, swap_rows(): return lax.all_to_all(buffer, 'dp', split_axis=0, concat_axis=0, tiled=True)  9.13 us
    another operation x6, local copies, waits for them, and re-layouts  8.59 us
  transfers between devices with their start and end apart: 4, of which 4 were waited for; matrix products, arithmetic and copies ran while one was open for 2% of the time, Pallas kernels for 0%

profile of v1, /device:TPU:0, one launch (start us, length us, event | category | flops | bytes accessed | tf_op | source)
XLA Modules:
  0.0 395.5 jit_solution(7527070246258354773)
XLA Ops:
  8.9 1.3 fusion.104
  11.0 1.2 copy.88
  12.3 9.7 %scatter_fusion = bf16[8,10,4096]{2,0,1:T(8,128)(2,1)S(1)} fusion(bf16[8,10,4096]{2,0,1:T(8,128)(2,1)S(1)} %broadcast.348.clone, s32[64]{0:T(128)S(1)} %get-tuple-element.15, bf16[64,4096]{1,0:T(8,128)(2,1)S(1)} %bitcast.217), kind=kCustom, calls=%fused_computation.8 | custom fusion | bytes 1573376 | tf_op jit(solution)/shard_map/scatter | solution.py:49
  22.0 1.4 copy.60
  23.4 5.2 %all-to-all-start = ((bf16[8,10,4096]{2,1,0:T(8,128)(2,1)}), bf16[8,10,4096]{2,1,0:T(8,128)(2,1)S(1)}, u32[]{:S(2)}, u32[]{:S(2)}) async-start(bf16[8,10,4096]{2,1,0:T(8,128)(2,1)} %copy.60), calls=%async_computation | async-start | bytes 2097152 | tf_op jit(solution)/shard_map/all_to_all | solution.py:14
  28.8 15.1 %all-to-all-done = bf16[8,10,4096]{2,1,0:T(8,128)(2,1)S(1)} async-done(((bf16[8,10,4096]{2,1,0:T(8,128)(2,1)}), bf16[8,10,4096]{2,1,0:T(8,128)(2,1)S(1)}, u32[]{:S(2)}, u32[]{:S(2)}) %all-to-all-start) | async-done | bytes 655392 | tf_op jit(solution)/shard_map/all_to_all | solution.py:14
  44.3 2.2 gather_fusion.2
  49.5 8.2 %all_gather.15 = bf16[512,128]{1,0:T(8,128)(2,1)S(1)} all-gather(bf16[64,128]{1,0:T(8,128)(2,1)S(1)} %copy-done.22), channel_id=1, replica_groups=mesh['dp'=8,'mp'=4] {'dp'}, dimensions={0}, use_global_device_ids=true | all-gather | bytes 147456 | tf_op jit(solution)/shard_map/all_gather | solution.py:23
  58.0 1.2 gather_fusion.4
  59.2 1.2 gather_fusion.3
  61.1 31.9 %all-gather.3.cloned.1.call-done = bf16[64,64,256]{2,1,0:T(8,128)(2,1)} async-done(((bf16[64,16,256]{2,1,0:T(8,128)(2,1)}), bf16[64,64,256]{2,1,0:T(8,128)(2,1)}) %all-gather.3.cloned.1.call-update) | async-done | bytes 2097168 | tf_op jit(solution)/shard_map/all_gather | solution.py:61
  93.0 2.4 convert_reduce_fusion
  95.4 3.1 broadcast_subtract_fusion
  98.6 2.5 fusion.10
  103.1 2.1 reshape.404
  105.2 2.2 reshape.403
  107.3 1.5 copy.87
  108.9 3.7 fusion.132
  112.6 5.0 %fusion.26 = (f32[64,64]{1,0:T(8,128)S(1)}, f32[64,64,64]{1,2,0:T(8,128)S(1)}) fusion(f32[64,64]{1,0:T(8,128)S(1)} %copy-done.20, bf16[64,64,64]{1,0,2:T(8,128)(2,1)S(1)} %copy-done.9, bf16[64,64,64]{1,0,2:T(8,128)(2,1)S(1)} %copy-done.7), kind=kOutput, calls=%fused_computation.48 | convolution fusion | flops 34336768 | bytes 2129920 | tf_op jit(solution)/shard_map/sthc,srhc->shtr/dot_general | solution.py:84
  117.7 1.3 fusion.44
  121.3 1.4 copy-done.4
  122.7 1.9 convolution_add_fusion.1
  124.7 2.1 fusion.133
  126.8 14.9 %all-gather = f32[256,256]{1,0:T(8,128)} all-gather(f32[64,256]{1,0:T(8,128)S(1)} %bitcast.222), channel_id=2, replica_groups=mesh['dp'=8,'mp'=4] {'mp'}, dimensions={0}, use_global_device_ids=true | all-gather | bytes 327680 | tf_op jit(solution)/shard_map/all_gather | solution.py:112
  141.7 1.6 reduce_sum.141
  147.4 1.6 convolution_convert_fusion
  149.0 2.7 reshape.407
  151.7 3.8 fusion.58
  155.5 3.4 fusion.45
  158.9 6.9 %fusion.49 = bf16[64,64,1,64]{1,3,0,2:T(8,128)(2,1)} fusion(f32[64,64,64]{1,2,0:T(8,128)} %fusion.58, bf16[64,64,64]{1,0,2:T(8,128)(2,1)} %reshape.404, f32[64,64,64]{1,2,0:T(8,128)} %copy-done.32, f32[64,64]{1,0:T(8,128)} %copy-done.34, f32[64,64]{1,0:T(8,128)} %fusion.80), kind=kOutput, calls=%fused_computation.64 | convolution fusion | flops 36704320 | bytes 3178496 | tf_op jit(solution)/shard_map/shtr,srhc->sthc/dot_general | solution.py:157
  165.8 7.7 %fusion.46 = bf16[64,64,1,64]{1,3,0,2:T(8,128)(2,1)} fusion(f32[64,64,64]{1,2,0:T(8,128)} %fusion.58, bf16[64,64,64]{1,0,2:T(8,128)(2,1)S(1)} %copy-done.8, f32[64,64,64]{1,2,0:T(8,128)} %copy-done.32, f32[64,64]{1,0:T(8,128)} %copy-done.34, f32[64,64]{1,0:T(8,128)} %fusion.80), kind=kOutput, calls=%fused_computation.63 | convolution fusion | flops 36704320 | bytes 3178496 | tf_op jit(solution)/shard_map/shtr,sthc->srhc/dot_general | solution.py:160
  173.5 1.9 copy.77
  175.4 1.6 stack.14
  177.0 1.9 copy.74
  178.9 1.6 stack.13
  180.6 1.9 copy.71
  182.5 1.6 stack.12
  184.1 4.2 %convolution_bitcast_fusion = f32[4096,256]{1,0:T(8,128)} fusion(bf16[3,256,64]{1,2,0:T(8,128)(2,1)} %param.17, bf16[1,4096,64]{1,2,0:T(8,128)(2,1)} %stack.14, bf16[1,4096,64]{1,2,0:T(8,128)(2,1)} %stack.13, bf16[1,4096,64]{1,2,0:T(8,128)(2,1)} %stack.12), kind=kOutput, calls=%fused_computation.14 | convolution fusion | flops 404226048 | bytes 5865472 | tf_op jit(solution)/shard_map/jrf,jdf->rd/dot_general | solution.py:164
  188.2 7.0 %convolution_add_fusion = f32[4096,256]{1,0:T(8,128)} fusion(f32[4096,256]{1,0:T(8,128)} %convolution_bitcast_fusion, bf16[256,256]{1,0:T(8,128)(2,1)S(1)} %copy-done.13, f32[4096,256]{1,0:T(8,128)} %fusion.132, bf16[4096,256]{1,0:T(8,128)(2,1)S(1)} %fusion.8, bf16[256,256]{1,0:T(8,128)(2,1)S(1)} %copy-done), kind=kOutput, calls=%fused_computation.13 | convolution fusion | flops 1095761920 | bytes 14942208 | tf_op jit(solution)/shard_map/rf,df->rd/dot_general | solution.py:166
  195.4 153.8 %all-reduce.2.cloned.1.call-done = f32[64,64,256]{2,1,0:T(8,128)} async-done(((f32[64,64,256]{2,1,0:T(8,128)}), f32[64,64,256]{2,1,0:T(8,128)}) %all-reduce.2.cloned.1.call-update) | async-done | bytes 4194320 | tf_op jit(solution)/shard_map/psum | solution.py:173
  349.2 2.1 dynamic-slice_reduce_fusion
  351.3 2.0 multiply_add_fusion
  354.1 9.7 %scatter_fusion.1 = bf16[8,10,4096]{2,0,1:T(8,128)(2,1)S(1)} fusion(bf16[8,10,4096]{2,0,1:T(8,128)(2,1)S(1)} %broadcast.348, s32[64]{0:T(128)S(1)} %get-tuple-element.16, bf16[64,4096]{1,0:T(8,128)(2,1)S(1)} %multiply_convert_fusion.3), kind=kCustom, calls=%fused_computation.9 | custom fusion | bytes 1573376 | tf_op jit(solution)/shard_map/scatter | solution.py:184
  363.8 1.4 copy.78
  365.2 3.9 all-to-all-start.1
  371.5 13.0 %all-to-all-done.1 = bf16[8,10,4096]{2,1,0:T(8,128)(2,1)S(1)} async-done(((bf16[8,10,4096]{2,1,0:T(8,128)(2,1)}), bf16[8,10,4096]{2,1,0:T(8,128)(2,1)S(1)}, u32[]{:S(2)}, u32[]{:S(2)}) %all-to-all-start.1) | async-done | bytes 655392 | tf_op jit(solution)/shard_map/all_to_all | solution.py:14
  384.9 2.2 gather_fusion.5
  387.2 1.2 bitcast_add_fusion
  (136 shorter events, 19.2 us)
Async XLA Ops:
  7.2 114.2 %copy-start = (bf16[256,256]{1,0:T(8,128)(2,1)S(1)}, bf16[256,256]{1,0:T(8,128)(2,1)}, u32[]{:S(2)}) copy-start(bf16[256,256]{1,0:T(8,128)(2,1)} %param.20) | copy-start | bytes 393220
  22.0 6.8 %copy-start.30 = (s32[64]{0:T(128)S(1)}, s32[64]{0:T(128)}, u32[]{:S(2)}) copy-start(s32[64]{0:T(128)} %param.15) | copy-start | bytes 772
  23.4 20.6 %all-to-all-start = ((bf16[8,10,4096]{2,1,0:T(8,128)(2,1)}), bf16[8,10,4096]{2,1,0:T(8,128)(2,1)S(1)}, u32[]{:S(2)}, u32[]{:S(2)}) async-start(bf16[8,10,4096]{2,1,0:T(8,128)(2,1)} %copy.60), calls=%async_computation | async-start | bytes 2097152 | tf_op jit(solution)/shard_map/all_to_all | solution.py:14
  28.6 64.4 %all-gather.3.cloned.1.call-start = ((), (), s32[]{:S(2)}) async-start(), calls=%async_computation.2 | async-start | bytes 2621440 | tf_op jit(solution)/shard_map/all_gather | solution.py:61
  28.8 17.9 %copy-start.26 = (f32[64]{0:T(128)}, f32[64]{0:T(128)S(1)}, u32[]{:S(2)}) copy-start(f32[64]{0:T(128)S(1)} %get-tuple-element.21) | copy-start | bytes 772
  28.8 17.9 %copy-start.28 = (f32[64]{0:T(128)}, f32[64]{0:T(128)S(1)}, u32[]{:S(2)}) copy-start(f32[64]{0:T(128)S(1)} %get-tuple-element.20) | copy-start | bytes 772
  44.3 2.4 copy-start.6
  46.5 1.3 copy-start.1
  46.5 3.0 copy-start.22
  47.8 301.4 %all-reduce.2.cloned.1.call-start = ((), (), s32[]{:S(2)}) async-start(), calls=%async_computation.3 | async-start | bytes 8388608 | tf_op jit(solution)/shard_map/psum | solution.py:173
  93.0 2.4 copy-start.2
  98.6 2.5 copy-start.16
  108.8 3.8 copy-start.7
  108.8 3.8 copy-start.9
  108.9 3.8 copy-start.20
  117.7 1.4 copy-start.32
  117.7 1.4 copy-start.34
  119.0 1.5 copy-start.14
  120.6 2.2 copy-start.4
  124.7 18.7 %copy-start.3 = (bf16[64,64,256]{2,1,0:T(8,128)(2,1)S(1)}, bf16[64,64,256]{2,1,0:T(8,128)(2,1)}, u32[]{:S(2)}) copy-start(bf16[64,64,256]{2,1,0:T(8,128)(2,1)} %all-gather.3.cloned.1.call-done) | copy-start | bytes 6291460
  126.8 17.5 %copy-start.10 = (bf16[256,128]{1,0:T(8,128)(2,1)S(1)}, bf16[256,128]{1,0:T(8,128)(2,1)}, u32[]{:S(2)}) copy-start(bf16[256,128]{1,0:T(8,128)(2,1)} %param.21) | copy-start | bytes 196612
  143.3 1.0 copy-start.12
  143.3 1.9 copy-start.18
  143.3 1.9 copy-start.19
  143.3 3.0 copy-start.11
  143.4 3.3 copy-start.17
  144.3 3.1 copy-start.15
  145.2 1.1 copy-start.23
  151.7 3.8 copy-start.5
  151.7 3.8 copy-start.21
  151.7 3.8 copy-start.33
  151.7 3.8 copy-start.35
  158.9 6.9 %copy-start.8 = (bf16[64,64,64]{1,0,2:T(8,128)(2,1)S(1)}, bf16[64,64,64]{1,0,2:T(8,128)(2,1)}, u32[]{:S(2)}) copy-start(bf16[64,64,64]{1,0,2:T(8,128)(2,1)} %reshape.403) | copy-start | bytes 1572868
  184.1 4.2 %copy-start.13 = (bf16[256,256]{1,0:T(8,128)(2,1)S(1)}, bf16[256,256]{1,0:T(8,128)(2,1)}, u32[]{:S(2)}) copy-start(bf16[256,256]{1,0:T(8,128)(2,1)} %param.19) | copy-start | bytes 393220
  351.3 2.6 copy-start.27
  363.8 5.4 %copy-start.25 = (s32[64,1,1]{0,2,1:T(1,128)S(1)}, s32[64,1,1]{0,2,1:T(1,128)}, u32[]{:S(2)}) copy-start(s32[64,1,1]{0,2,1:T(1,128)} %get-tuple-element.5) | copy-start | bytes 772
  363.8 7.2 %copy-start.24 = (f32[64]{0:T(128)S(1)}, f32[64]{0:T(128)}, u32[]{:S(2)}) copy-start(f32[64]{0:T(128)} %copy-done.23) | copy-start | bytes 772
  363.8 7.2 %copy-start.31 = (s32[64]{0:T(128)S(1)}, s32[64]{0:T(128)}, u32[]{:S(2)}) copy-start(s32[64]{0:T(128)} %param.15) | copy-start | bytes 772
  365.2 19.3 %all-to-all-start.1 = ((bf16[8,10,4096]{2,1,0:T(8,128)(2,1)}), bf16[8,10,4096]{2,1,0:T(8,128)(2,1)S(1)}, u32[]{:S(2)}, u32[]{:S(2)}) async-start(bf16[8,10,4096]{2,1,0:T(8,128)(2,1)} %copy.78), calls=%async_computation.1 | async-start | bytes 2097152 | tf_op jit(solution)/shard_map/all_to_all | solution.py:14
  384.9 2.4 copy-start.29
Sparse Core Ops, SparseCore 0:
  47.9 45.0 all-gather.2
  195.4 153.8 all-reduce.1
